TPU v7x, 512 devices: a whole 4x4x16 slice. The times are simulated.
512 devices in a mesh: slab: 16 (over z_hi, x), seq: 32 (over y, z_lo, core).
Axes of the slice: x: 4, y: 4, z: 16 (z_hi: 4, z_lo: 4; z = z_hi * 4 + z_lo), core: 2. Of those that a mesh axis runs over, the one named last changes fastest.
Arguments:
- video_tokens: bfloat16 [512, 512, 1152], P(('slab', 'seq')), may hold values from -40 to 40
- modulation: float32 [512, 3, 1152], P(('slab', 'seq')), may hold values from -3 to 3
- qkv_weight: bfloat16 [1152, 3456], P(None, 'seq'), may hold values from -1.5 to 1.5
- out_weight: bfloat16 [1152, 1152], P(None, 'seq'), may hold values from -0.1875 to 0.1875
Outputs:
- restored: bfloat16 [512, 512, 1152], P(('slab', 'seq'))
All inputs are finite; a program needn't handle non-finite values.
Results may differ from a plain program's by a relative error of at most 0.004.
Values may be sent and summed in bfloat16 or wider, within the bound.
A program may use at most 128 MiB of HBM per device.

v0:
```python
import jax
import jax.numpy as jnp
from jax import lax
from jax.sharding import PartitionSpec as P

H = 16
FRS = 32


epsilon = 1e-06


def shifted_2(value, axis, steps):
    count = lax.axis_size(axis)
    pairs = [(source, (source + steps) % count) for source in range(count)]
    return lax.ppermute(value, axis, pairs)


def modulate(tokens, modulation):
    values = tokens.astype(jnp.float32)
    average = jnp.mean(values, axis=-1, keepdims=True)
    centered = values - average
    variance = jnp.mean(centered * centered, axis=-1, keepdims=True)
    normed = centered * lax.rsqrt(variance + epsilon)
    return (normed * (1.0 + modulation[:, 1][:, None, :]) + modulation[:, 0][:, None, :]).astype(
        jnp.bfloat16
    )


def attend(queries, key_rows, value_rows):
    scores = jnp.einsum("wtphd,wsphd->wphts", queries, key_rows, preferred_element_type=jnp.float32)
    scores = scores * queries.shape[-1] ** (-0.5)
    scores = scores - jnp.max(scores, axis=-1, keepdims=True)
    exponent = jnp.exp(scores)
    softmaxed = (exponent / jnp.sum(exponent, axis=-1, keepdims=True)).astype(jnp.bfloat16)
    result = jnp.einsum(
        "wphts,wsphd->wtphd", softmaxed, value_rows, preferred_element_type=jnp.float32
    )
    return result.astype(jnp.bfloat16)


def per_device(video_tokens, modulation, qkv_weight, out_weight):
    width = video_tokens.shape[2]
    head_size = width // H
    heads_half = H // 2
    normed = modulate(video_tokens, modulation)
    position_major = lax.all_to_all(normed, "seq", split_axis=1, concat_axis=0, tiled=True)
    window_len = position_major.shape[0]
    pos_dev = position_major.shape[1]
    half_frames = FRS // 2
    token_rows = position_major.reshape(window_len * pos_dev, width)
    projected = jnp.dot(
        token_rows,
        lax.all_gather(qkv_weight, "seq", axis=1, tiled=True),
        preferred_element_type=jnp.float32,
    ).astype(jnp.bfloat16)
    grouped = projected.reshape(window_len, pos_dev, 6, heads_half, head_size)
    windowed = attend(grouped[None, :, :, 0], grouped[None, :, :, 1], grouped[None, :, :, 2])[0]
    shifted_group = grouped[:, :, 3:]
    arrived = shifted_2(shifted_group[half_frames:], "slab", 1)
    joined = jnp.concatenate([arrived, shifted_group[:half_frames]], axis=0)
    result = attend(joined[None, :, :, 0], joined[None, :, :, 1], joined[None, :, :, 2])[0]
    returned = shifted_2(result[:half_frames], "slab", -1)
    shifted = jnp.concatenate([result[half_frames:], returned], axis=0)
    attended = jnp.concatenate([windowed, shifted], axis=2).reshape(window_len * pos_dev, width)
    output_rows = jnp.dot(
        attended,
        lax.all_gather(out_weight, "seq", axis=1, tiled=True),
        preferred_element_type=jnp.float32,
    ).astype(jnp.bfloat16)
    frame_major = lax.all_to_all(
        output_rows.reshape(window_len, pos_dev, width),
        "seq",
        split_axis=0,
        concat_axis=1,
        tiled=True,
    )
    restored = video_tokens.astype(jnp.float32) + modulation[:, 2][:, None, :] * frame_major.astype(
        jnp.float32
    )
    return restored.astype(jnp.bfloat16)


def solution(mesh):
    return jax.shard_map(
        per_device,
        mesh=mesh,
        in_specs=(
            P(("slab", "seq"), None, None),
            P(("slab", "seq"), None, None),
            P(None, "seq"),
            P(None, "seq"),
        ),
        out_specs=P(("slab", "seq"), None, None),
        check_vma=False,
    )
```

profile of v0, /device:TPU:1, one launch (start us, length us, event | category | flops | bytes accessed | tf_op | source)
XLA Modules:
  0.0 406.9 jit_solution(7746840773859978478)
XLA Ops:
  12.9 8.8 %reduce.16 = bf16[512,1152]{1,0:T(8,128)(2,1)} reduce(bf16[512,1,1152]{2,1,0:T(2,128)(2,1)S(1)} %bitcast.87, bf16[]{:T(256)} %broadcast.83), dimensions={1}, to_apply=%bitcast.85.reduce_sub_computation | reduce | bytes 2359298
  21.6 3.8 reshape.173
  25.4 10.6 %all-to-all-start = ((bf16[32,2,9216]{2,1,0:T(2,128)(2,1)}), bf16[32,2,9216]{2,1,0:T(2,128)(2,1)S(1)}, u32[]{:S(2)}, u32[]{:S(2)}) async-start(bf16[32,2,9216]{2,1,0:T(2,128)(2,1)} %reshape.173), calls=%async_computation | async-start | bytes 2359296 | tf_op jit(solution)/shard_map/all_to_all | solution.py:47
  36.7 41.7 %all-to-all-done = bf16[32,2,9216]{2,1,0:T(2,128)(2,1)S(1)} async-done(((bf16[32,2,9216]{2,1,0:T(2,128)(2,1)}), bf16[32,2,9216]{2,1,0:T(2,128)(2,1)S(1)}, u32[]{:S(2)}, u32[]{:S(2)}) %all-to-all-start) | async-done | bytes 1179680 | tf_op jit(solution)/shard_map/all_to_all | solution.py:47
  78.4 3.4 reshape.174
  81.9 28.6 %all-gather.5.cloned.1.call-done = bf16[32,108,1152]{2,1,0:T(8,128)(2,1)} async-done(((bf16[1,108,1152]{2,1,0:T(8,128)(2,1)}), bf16[32,108,1152]{2,1,0:T(8,128)(2,1)}) %all-gather.5.cloned.1.call-update) | async-done | bytes 7962640 | tf_op jit(solution)/shard_map/all_gather | solution.py:54
  110.5 9.2 %reshape.167 = bf16[3456,1152]{1,0:T(8,128)(2,1)} reshape(bf16[32,108,1152]{2,1,0:T(8,128)(2,1)} %all-gather.5.cloned.1.call-done) | data formatting | bytes 15925248
  119.7 9.7 %convolution_convert_fusion = bf16[512,3456]{1,0:T(8,128)(2,1)} fusion(bf16[3456,1152]{1,0:T(8,128)(2,1)} %reshape.167, bf16[1,512,1152]{2,0,1:T(2,128)(2,1)S(1)} %bitcast.89), kind=kOutput, calls=%fused_computation.2 | convolution fusion | flops 4078632960 | bytes 12681216 | tf_op jit(solution)/shard_map/dot_general | solution.py:52
  129.4 13.7 %reshape.156 = bf16[32,16,6,8,72]{4,3,2,1,0:T(8,128)(2,1)} reshape(bf16[512,3456]{1,0:T(8,128)(2,1)} %convolution_convert_fusion) | data formatting | bytes 7077888 | tf_op jit(solution)/shard_map/reshape | solution.py:57
  143.0 2.5 fusion.24
  145.5 3.0 copy.45
  148.5 3.1 collective-permute-start
  151.6 25.3 %all-gather.7.cloned.1.call-done = bf16[32,36,1152]{2,1,0:T(8,128)(2,1)} async-done(((bf16[1,36,1152]{2,1,0:T(8,128)(2,1)}), bf16[32,36,1152]{2,1,0:T(8,128)(2,1)}) %all-gather.7.cloned.1.call-update) | async-done | bytes 2654224 | tf_op jit(solution)/shard_map/all_gather | solution.py:68
  176.9 5.1 %reshape.169 = bf16[1152,1152]{1,0:T(8,128)(2,1)} reshape(bf16[32,36,1152]{2,1,0:T(8,128)(2,1)} %all-gather.7.cloned.1.call-done) | data formatting | bytes 5308416
  182.1 3.7 fusion.23
  185.7 4.8 %fusion.26 = (f32[16,8,32]{2,1,0:T(8,128)S(1)}, f32[16,8,32,32]{2,3,1,0:T(8,128)}) fusion(bf16[32,16,1,8,72]{4,3,2,1,0:T(8,128)(2,1)} %get-tuple-element.9, bf16[32,16,1,8,72]{4,3,2,1,0:T(8,128)(2,1)} %get-tuple-element.10), kind=kOutput, calls=%fused_computation.56 | convolution fusion | flops 19267616 | bytes 1720320 | tf_op jit(solution)/shard_map/sub | solution.py:33
  190.5 66.1 %collective-permute-done = bf16[16,16,3,8,72]{4,0,3,1,2:T(8,128)(2,1)} collective-permute-done((bf16[16,16,3,8,72]{4,0,3,1,2:T(8,128)(2,1)}, bf16[16,16,3,8,72]{4,0,3,1,2:T(8,128)(2,1)}, u32[]{:S(2)}, u32[]{:S(2)}) %collective-permute-start) | collective-permute-done | bytes 884768 | tf_op jit(solution)/shard_map/ppermute | solution.py:16
  256.6 3.1 constant_dynamic-update-slice_fusion
  259.7 3.0 copy_dynamic-update-slice_fusion
  267.2 10.2 %collective-permute-start.1 = (bf16[16,16,8,72]{3,0,2,1:T(8,128)(2,1)S(1)}, bf16[16,16,8,72]{3,0,2,1:T(8,128)(2,1)S(1)}, u32[]{:S(2)}, u32[]{:S(2)}) collective-permute-start(bf16[16,16,8,72]{3,0,2,1:T(8,128)(2,1)S(1)} %get-tuple-element.14), channel_id=1, source_target_pairs={{0,480},{32,0},{64,32},{96,64},{128,96},{160,128},{192,160},{224,1... | collective-permute-start | bytes 884744 | tf_op jit(solution)/shard_map/ppermute | solution.py:16
  278.4 15.8 %collective-permute-done.1 = bf16[16,16,8,72]{3,0,2,1:T(8,128)(2,1)S(1)} collective-permute-done((bf16[16,16,8,72]{3,0,2,1:T(8,128)(2,1)S(1)}, bf16[16,16,8,72]{3,0,2,1:T(8,128)(2,1)S(1)}, u32[]{:S(2)}, u32[]{:S(2)}) %collective-permute-start.1) | collective-permute-done | bytes 294944 | tf_op jit(solution)/shard_map/ppermute | solution.py:16
  295.6 3.4 reshape.163
  299.0 4.0 convolution_convert_fusion.1
  303.0 95.8 %all_to_all.8 = bf16[32,16,1152]{2,1,0:T(8,128)(2,1)S(1)} all-to-all(bf16[32,16,1152]{2,1,0:T(8,128)(2,1)S(1)} %bitcast.90), channel_id=1, replica_groups=mesh['slab'=16,'seq'=32] {'seq'}, dimensions={0} | all-to-all | bytes 2359296 | tf_op jit(solution)/shard_map/all_to_all | solution.py:71
  (27 shorter events, 15.2 us)
Async XLA Ops:
  6.5 3.0 copy-start
  6.5 104.0 %all-gather.5.cloned.1.call-start = ((), (), s32[]{:S(2)}) async-start(), calls=%async_computation.2 | async-start | bytes 8515584 | tf_op jit(solution)/shard_map/all_gather | solution.py:54
  25.4 53.1 %all-to-all-start = ((bf16[32,2,9216]{2,1,0:T(2,128)(2,1)}), bf16[32,2,9216]{2,1,0:T(2,128)(2,1)S(1)}, u32[]{:S(2)}, u32[]{:S(2)}) async-start(bf16[32,2,9216]{2,1,0:T(2,128)(2,1)} %reshape.173), calls=%async_computation | async-start | bytes 2359296 | tf_op jit(solution)/shard_map/all_to_all | solution.py:47
  36.0 140.9 %all-gather.7.cloned.1.call-start = ((), (), s32[]{:S(2)}) async-start(), calls=%async_computation.3 | async-start | bytes 3041280 | tf_op jit(solution)/shard_map/all_gather | solution.py:68
  81.9 37.9 %copy-start.1 = (bf16[512,1,1152]{2,1,0:T(2,128)(2,1)S(1)}, bf16[512,1,1152]{2,1,0:T(2,128)(2,1)}, u32[]{:S(2)}) copy-start(bf16[512,1,1152]{2,1,0:T(2,128)(2,1)} %reshape.174) | copy-start | bytes 3538948
  148.5 108.1 %collective-permute-start = (bf16[16,16,3,8,72]{4,0,3,1,2:T(8,128)(2,1)}, bf16[16,16,3,8,72]{4,0,3,1,2:T(8,128)(2,1)}, u32[]{:S(2)}, u32[]{:S(2)}) collective-permute-start(bf16[16,16,3,8,72]{4,0,3,1,2:T(8,128)(2,1)} %copy.45), channel_id=1, source_target_pairs={{0,32},{32,64},{64,96},{96,128},{128,160},{160,192},{192,224},{224... | collective-permute-start | bytes 2654216 | tf_op jit(solution)/shard_map/ppermute | solution.py:16
  265.1 12.3 %copy-start.3 = (f32[16,8,32,32]{2,3,1,0:T(8,128)S(1)}, f32[16,8,32,32]{2,3,1,0:T(8,128)}, u32[]{:S(2)}) copy-start(f32[16,8,32,32]{2,3,1,0:T(8,128)} %get-tuple-element.18) | copy-start | bytes 1572868
  267.0 10.4 %copy-start.2 = (bf16[32,16,1,8,72]{4,3,2,1,0:T(8,128)(2,1)S(1)}, bf16[32,16,1,8,72]{4,3,2,1,0:T(8,128)(2,1)}, u32[]{:S(2)}) copy-start(bf16[32,16,1,8,72]{4,3,2,1,0:T(8,128)(2,1)} %get-tuple-element.8) | copy-start | bytes 1769476
  267.2 27.0 %collective-permute-start.1 = (bf16[16,16,8,72]{3,0,2,1:T(8,128)(2,1)S(1)}, bf16[16,16,8,72]{3,0,2,1:T(8,128)(2,1)S(1)}, u32[]{:S(2)}, u32[]{:S(2)}) collective-permute-start(bf16[16,16,8,72]{3,0,2,1:T(8,128)(2,1)S(1)} %get-tuple-element.14), channel_id=1, source_target_pairs={{0,480},{32,0},{64,32},{96,64},{128,96},{160,128},{192,160},{224,1... | collective-permute-start | bytes 884744 | tf_op jit(solution)/shard_map/ppermute | solution.py:16
Sparse Core Ops, SparseCore 0:
  9.5 100.9 all-gather.4
  112.7 64.2 all-gather.6
where the time goes:
time: 410 us; the launch traced here: 407 us
  waiting for transfers between devices  179 us (44%)
  blocking collectives  95.8 us (23%)
  local copies, waits for them, and re-layouts  57.2 us (14%)
  starting transfers between devices  23.9 us (6%)
  matrix products  23.7 us (6%)
  other arithmetic  13.9 us (3%)
  between operations  13.5 us (3%)
    all_to_all x1, blocking collectives, per_device(): lax.all_to_all(output_rows.reshape(window_len, pos_dev, width), 'seq', sp...  95.8 us
    ppermute x2, waiting for transfers between devices, shifted_2(): return lax.ppermute(value, axis, pairs)  81.9 us
    all_to_all x1, waiting for transfers between devices, per_device(): lax.all_to_all(normed, 'seq', split_axis=1, concat_axis=0, tiled=True)  41.7 us
    all_gather x1, waiting for transfers between devices, per_device(): lax.all_gather(qkv_weight, 'seq', axis=1, tiled=True)  28.6 us
    unnamed x15, local copies, waits for them, and re-layouts  28.1 us
    all_gather x1, waiting for transfers between devices, per_device(): lax.all_gather(out_weight, 'seq', axis=1, tiled=True)  25.3 us
    reshape x1, local copies, waits for them, and re-layouts, per_device(): grouped = projected.reshape(window_len, pos_dev, 6, heads_half, head_size)  13.7 us
    ppermute x2, starting transfers between devices, shifted_2(): return lax.ppermute(value, axis, pairs)  13.3 us
  transfers between devices with their start and end apart: 5, of which 5 were waited for; matrix products, arithmetic and copies ran while one was open for 18% of the time, Pallas kernels for 0%

commit v1 on v0

v1 whole, which is shorter than its diff:
```python
import functools

import jax
import jax.numpy as jnp
from jax import lax
from jax.experimental import pallas as pl
from jax.experimental.pallas import tpu as pltpu
from jax.sharding import PartitionSpec as P

D = 1152
HEAD = 72
GROUP = 576
WIDE = 640
NSEQ = 32
NSLAB = 16
QROWS = 108
OROWS = 36
MESH = pl.DeviceIdType.MESH
EPS = 1e-06
BF = jnp.bfloat16
F32 = jnp.float32


def dot_nt(a, b):
    return lax.dot_general(a, b, (((1,), (1,)), ((), ())), preferred_element_type=F32)


def kernel(
    tok_ref, mod_ref, qw_ref, ow_ref, out_ref,
    hbuf, xbuf, wq, wo, wt, wot, xa, xb, halo_l, halo_u,
    qs, kts, vs, att, att_b, edge, ret_l, ret_u, obuf,
    wrecv, zsend, ysend, xsend, ssend, lsem, tsend, trecv, hsem, rsem, osend, orecv,
):
    s = lax.axis_index("slab")
    j = lax.axis_index("seq")
    x = lax.rem(s, 4)
    zh = lax.div(s, 4)
    y = lax.div(j, 8)
    zl = lax.rem(lax.div(j, 2), 4)
    c = lax.rem(j, 2)
    even = lax.rem(x, 2) == 0
    odd = lax.rem(x, 2) == 1
    par = lax.rem(x, 2)

    def zdev(off):
        zz = lax.rem(zh * 4 + zl + off + 16, 16)
        return (lax.div(zz, 4) * 4 + x, y * 8 + lax.rem(zz, 4) * 2 + c)

    def ydev(off):
        return (s, lax.rem(y + off + 4, 4) * 8 + zl * 2 + c)

    def xdev(off):
        return (zh * 4 + lax.rem(x + off + 4, 4), j)

    sib = (s, y * 8 + zl * 2 + (1 - c))
    up = (lax.rem(s + 1, NSLAB), j)
    down = (lax.rem(s + NSLAB - 1, NSLAB), j)

    def rdma(src, dst, ssem, rsem_, dev):
        return pltpu.make_async_remote_copy(
            src_ref=src, dst_ref=dst, send_sem=ssem, recv_sem=rsem_,
            device_id=dev, device_id_type=MESH,
        )

    barrier = pltpu.get_barrier_semaphore()

    def greet(k, carry):
        pl.semaphore_signal(
            barrier, inc=1, device_id=(s, lax.rem(j + k, NSEQ)), device_id_type=MESH
        )
        return carry

    lax.fori_loop(1, NSEQ, greet, 0)
    for dev in (xdev(1), xdev(-1), zdev(1), zdev(-1), zdev(2), zdev(-2), up, down):
        pl.semaphore_signal(barrier, inc=1, device_id=dev, device_id_type=MESH)
    own_q = pltpu.make_async_copy(qw_ref, wq.at[j], lsem.at[0])
    own_o = pltpu.make_async_copy(ow_ref, wo.at[j], lsem.at[1])
    own_q.start()
    own_o.start()
    own_q.wait()
    own_o.wait()
    pl.semaphore_wait(barrier, NSEQ - 1 + 8)

    def slot(yo, zo):
        return lax.rem(y + yo, 4) * 8 + lax.rem(zl + zo, 4) * 2 + c

    def ship(q, sems, i, dev):
        rdma(wq.at[q], wq.at[q], sems.at[0, i], wrecv.at[0, q], dev).start()
        rdma(wo.at[q], wo.at[q], sems.at[1, i], wrecv.at[1, q], dev).start()

    def shipped(sems, i):
        rdma(wq.at[0], wq.at[0], sems.at[0, i], wrecv.at[0, 0], sib).wait_send()
        rdma(wo.at[0], wo.at[0], sems.at[1, i], wrecv.at[1, 0], sib).wait_send()

    def landed(q):
        rdma(wq.at[q], wq.at[q], zsend.at[0, 0], wrecv.at[0, q], sib).wait_recv()
        rdma(wo.at[q], wo.at[q], zsend.at[1, 0], wrecv.at[1, q], sib).wait_recv()

    za = par * 3
    zb = 1 + par
    oa = (1 - par) * 3
    ob = 2 - par
    plus = ((0, 0), (0, 2), (1, 1), (1, 3))

    @pl.when(even)
    def _():
        ship(j, zsend, 0, zdev(-1))

    @pl.when(odd)
    def _():
        ship(j, zsend, 0, zdev(1))
        ship(j, zsend, 1, zdev(-2))

    @pl.when(even)
    def _():
        ship(j, ysend, 0, ydev(1))
        ship(j, ysend, 1, ydev(-1))

    ship(j, ssend, 0, sib)

    shift = mod_ref[0:1, :]
    scale = 1.0 + mod_ref[1:2, :]

    def norm(i, carry):
        rows = pl.ds(pl.multiple_of(i * 32, 32), 32)
        values = tok_ref[rows, :].astype(F32)
        centered = values - jnp.mean(values, axis=-1, keepdims=True)
        variance = jnp.mean(centered * centered, axis=-1, keepdims=True)
        normed = centered * lax.rsqrt(variance + EPS) * scale + shift
        hbuf[pl.ds(i * 2, 2)] = normed.reshape(2, 2, 8, D).astype(BF)
        return carry

    lax.fori_loop(0, 16, norm, 0)

    def send_tokens(k, carry):
        d = lax.rem(j + k, NSEQ)
        rdma(hbuf.at[d], xbuf.at[j], tsend, trecv, (s, d)).start()
        return carry

    lax.fori_loop(1, NSEQ, send_tokens, 0)
    own_tok = pltpu.make_async_copy(hbuf.at[j], xbuf.at[j], lsem.at[2])
    own_tok.start()

    def x_ship(kind, yo, q):
        i = kind * 4 + yo
        ship(q, xsend, i, xdev(1 if (kind, yo) in plus else -1))

    q = slot(0, za)

    @pl.when(odd)
    def _():
        landed(q)
        ship(q, ysend, 0, ydev(1))
        ship(q, ysend, 1, ydev(-1))
        x_ship(0, 0, q)
        ship(q, ssend, 1, sib)

    q1 = slot(0, zb)
    landed(q1)
    ship(q1, ysend, 2, ydev(1))
    ship(q1, ysend, 3, ydev(-1))
    x_ship(1, 0, q1)
    ship(q1, ssend, 2, sib)
    n = 3
    for kind, yo in ((0, 3), (0, 1), (1, 1), (1, 3), (0, 2), (1, 2)):
        q = slot(yo, zb if kind else za)
        landed(q)
        if (kind, yo) == (0, 3):
            ship(q, ysend, 4, ydev(1))
        if (kind, yo) == (1, 1):
            ship(q, ysend, 5, ydev(-1))
        x_ship(kind, yo, q)
        ship(q, ssend, n, sib)
        n += 1

    q0 = slot(0, oa)

    @pl.when(even)
    def _():
        landed(q0)
        ship(q0, ssend, 1, sib)

    for kind, yo in ((1, 0), (0, 1), (0, 3), (1, 1), (1, 3), (0, 2), (1, 2)):
        q = slot(yo, ob if kind else oa)
        landed(q)
        ship(q, ssend, n, sib)
        n += 1

    own_tok.wait()
    rdma(xbuf.at[pl.ds(0, NSEQ - 1)], xbuf.at[pl.ds(0, NSEQ - 1)], tsend, trecv, sib).wait_recv()
    half_up = rdma(xbuf.at[pl.ds(16, 16), 0], halo_l, hsem.at[0], hsem.at[1], up)
    half_down = rdma(xbuf.at[pl.ds(0, 16), 1], halo_u, hsem.at[2], hsem.at[3], down)
    half_up.start()
    half_down.start()

    for b in range(2):
        rows = xbuf[:, b].astype(F32).reshape(256, D).astype(BF)
        xa[256 * b:256 * b + 256, :] = rows
    xb[128:256, :] = xa[0:128, :]
    xb[256:384, :] = xa[384:512, :]

    def other(i, carry):
        landed(i * 2 + 1 - c)
        return carry

    lax.fori_loop(0, 16, other, 0)
    for i in range(16):
        wt[216 * i:216 * i + 216, :] = jnp.concatenate([wq[2 * i], wq[2 * i + 1]], axis=0)
        wot[72 * i:72 * i + 72, :] = jnp.concatenate([wo[2 * i], wo[2 * i + 1]], axis=0)

    def project(g, rows_ref):
        base = 1728 * g
        vbase = 2816 if g else 1152
        rows = rows_ref[...]
        qs[...] = dot_nt(rows, wt[base:base + WIDE, :]).astype(BF)
        kts[...] = dot_nt(wt[base + GROUP:base + GROUP + WIDE, :], rows).astype(BF)
        vs[...] = dot_nt(rows, wt[vbase:vbase + WIDE, :]).astype(BF)

    def attend(g, store):
        phase = 64 * g
        row_id = lax.broadcasted_iota(jnp.int32, (256, 256), 0)
        col_id = lax.broadcasted_iota(jnp.int32, (256, 256), 1)
        same = lax.rem(row_id, 8) == lax.rem(col_id, 8)

        def block(b, carry):
            at = pl.ds(pl.multiple_of(b * 256, 256), 256)
            tiles = {}
            for h in range(8):
                lo = HEAD * h
                t0, t1 = lo // 128, (lo + HEAD - 1) // 128
                width = 128 * (t1 - t0 + 1)
                r = lax.broadcasted_iota(jnp.int32, (width, 256), 0) + t0 * 128
                keep = jnp.where((r >= lo) & (r < lo + HEAD), 1.0, 0.0).astype(BF)
                kt = kts[t0 * 128:t0 * 128 + width, at] * keep
                scores = jnp.dot(
                    qs[at, t0 * 128:t0 * 128 + width], kt, preferred_element_type=F32
                ) * (HEAD ** -0.5)
                scores = jnp.where(same, scores, -1e30)
                top = jnp.max(scores, axis=-1, keepdims=True)
                e = jnp.exp(scores - top)
                p = (e * (1.0 / jnp.sum(e, axis=-1, keepdims=True))).astype(BF)
                lo = HEAD * h + phase
                t0, t1 = lo // 128, (lo + HEAD - 1) // 128
                width = 128 * (t1 - t0 + 1)
                r = lax.broadcasted_iota(jnp.int32, (256, width), 1) + t0 * 128
                keep = jnp.where((r >= lo) & (r < lo + HEAD), 1.0, 0.0).astype(BF)
                v = vs[at, t0 * 128:t0 * 128 + width] * keep
                o = jnp.dot(p, v, preferred_element_type=F32)
                for t in range(t0, t1 + 1):
                    piece = o[:, (t - t0) * 128:(t - t0 + 1) * 128]
                    tiles[t] = tiles[t] + piece if t in tiles else piece
                for t in list(tiles):
                    if h == 7 or t < (HEAD * (h + 1) + phase) // 128:
                        store(at, t, tiles.pop(t).astype(BF))
            return carry

        lax.fori_loop(0, 2, block, 0)

    def store_a(at, t, value):
        if t < 4:
            att[at, t * 128:t * 128 + 128] = value
        else:
            edge[at, :] = value

    def store_b(at, t, value):
        att_b[at, t * 128:t * 128 + 128] = value

    project(0, xa)
    attend(0, store_a)

    half_up.wait()
    half_down.wait()
    xb[0:128, :] = halo_l[...].astype(F32).reshape(128, D).astype(BF)
    xb[384:512, :] = halo_u[...].astype(F32).reshape(128, D).astype(BF)
    project(1, xb)
    attend(1, store_b)

    back_l = rdma(att_b.at[pl.ds(0, 128)], ret_l, rsem.at[0], rsem.at[1], down)
    back_u = rdma(att_b.at[pl.ds(384, 128)], ret_u, rsem.at[2], rsem.at[3], up)
    back_l.start()
    back_u.start()
    back_l.wait()
    back_u.wait()
    for rows, part in (
        (slice(0, 128), att_b[128:256, :]),
        (slice(128, 256), ret_l[...]),
        (slice(256, 384), ret_u[...]),
        (slice(384, 512), att_b[256:384, :]),
    ):
        att[rows, 512:640] = edge[rows, :] + part[:, 0:128]
        att[rows, 640:1152] = part[:, 128:640]

    for b in range(2):
        result = dot_nt(att[256 * b:256 * b + 256, :], wot[...])
        obuf[:, b] = result.reshape(32, 8, D).astype(BF)

    def send_out(k, carry):
        d = lax.rem(j + k, NSEQ)
        rdma(obuf.at[d], out_ref.at[j], osend, orecv, (s, d)).start()
        return carry

    lax.fori_loop(1, NSEQ, send_out, 0)
    own_out = pltpu.make_async_copy(obuf.at[j], out_ref.at[j], lsem.at[2])
    own_out.start()

    shipped(zsend, 0)

    @pl.when(odd)
    def _():
        shipped(zsend, 1)
        shipped(xsend, 0)

    for i in range(6):
        shipped(ysend, i)
    for i in range(1, 8):
        shipped(xsend, i)
    for i in range(16):
        shipped(ssend, i)
    own_out.wait()
    many = pl.ds(0, NSEQ - 1)
    rdma(hbuf.at[many], xbuf.at[many], tsend, trecv, sib).wait_send()
    rdma(obuf.at[many], out_ref.at[many], osend, orecv, sib).wait_send()
    rdma(obuf.at[many], out_ref.at[many], osend, orecv, sib).wait_recv()


def per_device(video_tokens, modulation, qkv_weight, out_weight):
    vmem = pl.BlockSpec(memory_space=pltpu.VMEM)
    anywhere = pl.BlockSpec(memory_space=pl.ANY)
    projected = pl.pallas_call(
        kernel,
        out_shape=jax.ShapeDtypeStruct((NSEQ, 2, 8, D), BF),
        in_specs=[vmem, vmem, anywhere, anywhere],
        out_specs=anywhere,
        scratch_shapes=[
            pltpu.VMEM((NSEQ, 2, 8, D), BF),
            pltpu.VMEM((NSEQ, 2, 8, D), BF),
            pltpu.VMEM((NSEQ, QROWS, D), BF),
            pltpu.VMEM((NSEQ, OROWS, D), BF),
            pltpu.VMEM((3 * D, D), BF),
            pltpu.VMEM((D, D), BF),
            pltpu.VMEM((512, D), BF),
            pltpu.VMEM((512, D), BF),
            pltpu.VMEM((16, 8, D), BF),
            pltpu.VMEM((16, 8, D), BF),
            pltpu.VMEM((512, WIDE), BF),
            pltpu.VMEM((WIDE, 512), BF),
            pltpu.VMEM((512, WIDE), BF),
            pltpu.VMEM((512, D), BF),
            pltpu.VMEM((512, WIDE), BF),
            pltpu.VMEM((512, 128), BF),
            pltpu.VMEM((128, WIDE), BF),
            pltpu.VMEM((128, WIDE), BF),
            pltpu.VMEM((NSEQ, 2, 8, D), BF),
            pltpu.SemaphoreType.DMA((2, NSEQ)),
            pltpu.SemaphoreType.DMA((2, 2)),
            pltpu.SemaphoreType.DMA((2, 6)),
            pltpu.SemaphoreType.DMA((2, 8)),
            pltpu.SemaphoreType.DMA((2, 16)),
            pltpu.SemaphoreType.DMA((3,)),
            pltpu.SemaphoreType.DMA,
            pltpu.SemaphoreType.DMA,
            pltpu.SemaphoreType.DMA((4,)),
            pltpu.SemaphoreType.DMA((4,)),
            pltpu.SemaphoreType.DMA,
            pltpu.SemaphoreType.DMA,
        ],
        compiler_params=pltpu.CompilerParams(
            collective_id=0, has_side_effects=True, vmem_limit_bytes=60 * 2**20
        ),
    )(
        video_tokens.reshape(512, D),
        modulation.reshape(3, D),
        qkv_weight.T,
        out_weight.T,
    )
    frame_major = projected.reshape(1, 512, D)
    restored = video_tokens.astype(F32) + modulation[:, 2][:, None, :] * frame_major.astype(F32)
    return restored.astype(BF)


def solution(mesh):
    return jax.shard_map(
        per_device,
        mesh=mesh,
        in_specs=(
            P(("slab", "seq"), None, None),
            P(("slab", "seq"), None, None),
            P(None, "seq"),
            P(None, "seq"),
        ),
        out_specs=P(("slab", "seq"), None, None),
        check_vma=False,
    )
```

time: 410 us -> 147 us (0.36)
  waiting for transfers between devices: 179 us -> 0 us
  Pallas kernels: 0 us -> 140 us
  blocking collectives: 95.8 us -> 0 us
  local copies, waits for them, and re-layouts: 57.2 us -> 2.03 us
  starting transfers between devices: 23.9 us -> 0 us
  matrix products: 23.7 us -> 0 us
  between operations: 13.5 us -> 0.02 us
  other arithmetic: 13.9 us -> 2.64 us
    pallas_call x0 -> x1, Pallas kernels: none -> 140 us  [per_device(): pl.pallas_call(kernel, out_shape=jax.ShapeDtypeStruct((NSEQ, 2, 8, D), BF...]
    all_to_all x1 -> x0, blocking collectives: 95.8 us -> none  [per_device(): lax.all_to_all(output_rows.reshape(window_len, pos_dev, width), 'seq', sp...]
    ppermute x2 -> x0, waiting for transfers between devices: 81.9 us -> none  [shifted_2(): return lax.ppermute(value, axis, pairs)]
    all_gather x2 -> x0, waiting for transfers between devices: 53.9 us -> none  [the longest x1 28.6 us: per_device(): lax.all_gather(qkv_weight, 'seq', axis=1, tiled=True)]
    all_to_all x1 -> x0, waiting for transfers between devices: 41.7 us -> none  [per_device(): lax.all_to_all(normed, 'seq', split_axis=1, concat_axis=0, tiled=True)]
    unnamed x15 -> x3, local copies, waits for them, and re-layouts: 28.1 us -> 1.33 us
    reshape x2 -> x0, local copies, waits for them, and re-layouts: 17.1 us -> none  [the longest x1 13.7 us: per_device(): grouped = projected.reshape(window_len, pos_dev, 6, heads_half, head_size)]
    dot_general x4 -> x0, matrix products: 16.5 us -> none  [the longest x1 9.65 us: per_device(): jnp.dot(token_rows, lax.all_gather(qkv_weight, 'seq', axis=1, tiled=True)...]
  transfers between devices with their start and end apart: 5 -> 0, of which waited for: 5 -> 0; matrix products, arithmetic and copies ran while one was open for 18% -> 0% of each run, Pallas kernels for 0% -> 0%
where the time goes in v1:
time: 147 us; the launch traced here: 145 us
  Pallas kernels  140 us (95%)
  other arithmetic  2.64 us (2%)
  local copies, waits for them, and re-layouts  2.03 us (1%)
    pallas_call x1, Pallas kernels, per_device(): pl.pallas_call(kernel, out_shape=jax.ShapeDtypeStruct((NSEQ, 2, 8, D), BF...  140 us

profile of v1, /device:TPU:1, one launch (start us, length us, event | category | flops | bytes accessed | tf_op | source)
XLA Modules:
  0.0 145.0 jit_solution(17704503185579533742)
XLA Ops:
  0.0 0.7 slice_reduce_fusion
  0.7 1.3 copy.7
  2.0 0.0 copy-start
  2.0 140.3 %shard_map.46 = bf16[32,2,8,1152]{3,2,1,0:T(8,128)(2,1)} custom-call(bf16[512,1152]{1,0:T(8,128)(2,1)} %bitcast.8, f32[3,1152]{1,0:T(4,128)} %bitcast.12, bf16[108,1152]{1,0:T(8,128)(2,1)} %bitcast.10, bf16[36,1152]{1,0:T(8,128)(2,1)} %bitcast.11), custom_call_target="tpu_custom_call" | custom-call | tf_op jit(solution)/shard_map/pallas_call | solution.py:329
  142.3 0.0 copy-done
  142.3 2.6 %fusion.1 = bf16[1,512,1152]{2,1,0:T(8,128)(2,1)} fusion(bf16[1,512,1152]{2,1,0:T(8,128)(2,1)} %bitcast.9, bf16[1,512,1152]{2,1,0:T(8,128)(2,1)S(1)} %copy-done, f32[1152]{0:T(1024)S(1)} %slice_reduce_fusion), kind=kLoop, calls=%fused_computation.2 | loop fusion | flops 2949120 | bytes 3543552 | tf_op jit(solution)/shard_map/convert_element_type | solution.py:378
Async XLA Ops:
  2.0 140.3 %copy-start = (bf16[1,512,1152]{2,1,0:T(8,128)(2,1)S(1)}, bf16[1,512,1152]{2,1,0:T(8,128)(2,1)}, u32[]{:S(2)}) copy-start(bf16[1,512,1152]{2,1,0:T(8,128)(2,1)} %param.4) | copy-start | bytes 3538948

commit v2 on v1

--- a/solution.py
+++ b/solution.py
@@ -29,7 +29,7 @@
     tok_ref, mod_ref, qw_ref, ow_ref, out_ref,
     hbuf, xbuf, wq, wo, wt, wot, xa, xb, halo_l, halo_u,
     qs, kts, vs, att, att_b, edge, ret_l, ret_u, obuf,
-    wrecv, zsend, ysend, xsend, ssend, lsem, tsend, trecv, hsem, rsem, osend, orecv,
+    wrecv, zsend, ysend, xsend, ssend, lsem, tsend, trecv, hsend, hrecv, osend, orecv,
 ):
     s = lax.axis_index("slab")
     j = lax.axis_index("seq")
@@ -53,9 +53,6 @@
         return (zh * 4 + lax.rem(x + off + 4, 4), j)
 
     sib = (s, y * 8 + zl * 2 + (1 - c))
-    up = (lax.rem(s + 1, NSLAB), j)
-    down = (lax.rem(s + NSLAB - 1, NSLAB), j)
-
     def rdma(src, dst, ssem, rsem_, dev):
         return pltpu.make_async_remote_copy(
             src_ref=src, dst_ref=dst, send_sem=ssem, recv_sem=rsem_,
@@ -71,30 +68,48 @@
         return carry
 
     lax.fori_loop(1, NSEQ, greet, 0)
-    for dev in (xdev(1), xdev(-1), zdev(1), zdev(-1), zdev(2), zdev(-2), up, down):
+    for dev in (xdev(1), xdev(-1), xdev(2), zdev(1), zdev(-1), zdev(2), zdev(-2)):
         pl.semaphore_signal(barrier, inc=1, device_id=dev, device_id_type=MESH)
+    for q in range(4):
+        for block in (zh + 1, zh + 3):
+            pl.semaphore_signal(
+                barrier, inc=1, device_id=(lax.rem(block, 4) * 4 + q, j), device_id_type=MESH
+            )
     own_q = pltpu.make_async_copy(qw_ref, wq.at[j], lsem.at[0])
     own_o = pltpu.make_async_copy(ow_ref, wo.at[j], lsem.at[1])
     own_q.start()
     own_o.start()
+
+    shift = mod_ref[0]
+    scale = 1.0 + mod_ref[1]
+
+    def norm(i, carry):
+        rows = pl.ds(pl.multiple_of(i * 64, 64), 64)
+        values = tok_ref[rows, :].astype(F32)
+        centered = values - jnp.mean(values, axis=-1, keepdims=True)
+        variance = jnp.mean(centered * centered, axis=-1, keepdims=True)
+        normed = centered * lax.rsqrt(variance + EPS) * scale + shift
+        hbuf[pl.ds(i * 4, 4)] = normed.reshape(4, 2, 8, D).astype(BF)
+        return carry
+
+    lax.fori_loop(0, 8, norm, 0)
     own_q.wait()
     own_o.wait()
-    pl.semaphore_wait(barrier, NSEQ - 1 + 8)
+    pl.semaphore_wait(barrier, NSEQ - 1 + 15)
 
     def slot(yo, zo):
         return lax.rem(y + yo, 4) * 8 + lax.rem(zl + zo, 4) * 2 + c
 
-    def ship(q, sems, i, dev):
-        rdma(wq.at[q], wq.at[q], sems.at[0, i], wrecv.at[0, q], dev).start()
-        rdma(wo.at[q], wo.at[q], sems.at[1, i], wrecv.at[1, q], dev).start()
-
-    def shipped(sems, i):
-        rdma(wq.at[0], wq.at[0], sems.at[0, i], wrecv.at[0, 0], sib).wait_send()
-        rdma(wo.at[0], wo.at[0], sems.at[1, i], wrecv.at[1, 0], sib).wait_send()
-
-    def landed(q):
-        rdma(wq.at[q], wq.at[q], zsend.at[0, 0], wrecv.at[0, q], sib).wait_recv()
-        rdma(wo.at[q], wo.at[q], zsend.at[1, 0], wrecv.at[1, q], sib).wait_recv()
+    bufs = (wq, wo)
+
+    def ship(t, q, sems, i, dev):
+        rdma(bufs[t].at[q], bufs[t].at[q], sems.at[t, i], wrecv.at[t, q], dev).start()
+
+    def shipped(t, sems, i):
+        rdma(bufs[t].at[0], bufs[t].at[0], sems.at[t, i], wrecv.at[t, 0], sib).wait_send()
+
+    def landed(t, q):
+        rdma(bufs[t].at[q], bufs[t].at[q], zsend.at[t, 0], wrecv.at[t, q], sib).wait_recv()
 
     za = par * 3
     zb = 1 + par
@@ -102,35 +117,116 @@
     ob = 2 - par
     plus = ((0, 0), (0, 2), (1, 1), (1, 3))
 
-    @pl.when(even)
-    def _():
-        ship(j, zsend, 0, zdev(-1))
-
-    @pl.when(odd)
-    def _():
-        ship(j, zsend, 0, zdev(1))
-        ship(j, zsend, 1, zdev(-2))
-
-    @pl.when(even)
-    def _():
-        ship(j, ysend, 0, ydev(1))
-        ship(j, ysend, 1, ydev(-1))
-
-    ship(j, ssend, 0, sib)
-
-    shift = mod_ref[0:1, :]
-    scale = 1.0 + mod_ref[1:2, :]
-
-    def norm(i, carry):
-        rows = pl.ds(pl.multiple_of(i * 32, 32), 32)
-        values = tok_ref[rows, :].astype(F32)
-        centered = values - jnp.mean(values, axis=-1, keepdims=True)
-        variance = jnp.mean(centered * centered, axis=-1, keepdims=True)
-        normed = centered * lax.rsqrt(variance + EPS) * scale + shift
-        hbuf[pl.ds(i * 2, 2)] = normed.reshape(2, 2, 8, D).astype(BF)
-        return carry
-
-    lax.fori_loop(0, 16, norm, 0)
+    def x_ship(t, kind, yo, q):
+        ship(t, q, xsend, kind * 4 + yo, xdev(1 if (kind, yo) in plus else -1))
+
+    def stage_z(t):
+        @pl.when(even)
+        def _():
+            ship(t, j, zsend, 0, zdev(-1))
+            ship(t, j, ysend, 0, ydev(1))
+            ship(t, j, ysend, 1, ydev(-1))
+
+        @pl.when(odd)
+        def _():
+            ship(t, j, zsend, 1, zdev(-2))
+            ship(t, j, zsend, 0, zdev(1))
+
+        ship(t, j, ssend, 0, sib)
+
+    def stage_ab(t):
+        @pl.when(odd)
+        def _():
+            q = slot(0, za)
+            landed(t, q)
+            ship(t, q, ysend, 0, ydev(1))
+            ship(t, q, ysend, 1, ydev(-1))
+            x_ship(t, 0, 0, q)
+            ship(t, q, ssend, 1, sib)
+
+        q = slot(0, zb)
+        landed(t, q)
+        ship(t, q, ysend, 2, ydev(1))
+        ship(t, q, ysend, 3, ydev(-1))
+        x_ship(t, 1, 0, q)
+        ship(t, q, ssend, 2, sib)
+
+    near = ((0, 3), (0, 1), (1, 1), (1, 3))
+    far = ((0, 2), (1, 2))
+
+    def stage_y(t, which, n):
+        for kind, yo in which:
+            q = slot(yo, zb if kind else za)
+            landed(t, q)
+            if (kind, yo) == (0, 3):
+                ship(t, q, ysend, 4, ydev(1))
+            if (kind, yo) == (1, 1):
+                ship(t, q, ysend, 5, ydev(-1))
+            x_ship(t, kind, yo, q)
+            ship(t, q, ssend, n, sib)
+            n += 1
+
+    def stage_x(t):
+        @pl.when(even)
+        def _():
+            q = slot(0, oa)
+            landed(t, q)
+            ship(t, q, ssend, 1, sib)
+
+        n = 9
+        for kind, yo in ((1, 0), (0, 1), (0, 3), (1, 1), (1, 3), (0, 2), (1, 2)):
+            q = slot(yo, ob if kind else oa)
+            landed(t, q)
+            ship(t, q, ssend, n, sib)
+            n += 1
+
+    def stage_s(t):
+        def other(i, carry):
+            landed(t, i * 2 + 1 - c)
+            return carry
+
+        lax.fori_loop(0, 16, other, 0)
+
+    last = lax.div(x, 3)
+    first = lax.div(3 - x, 3)
+
+    def go_up(pieces, buf, ss, rs):
+        for q in range(4):
+            dest = (1 - last) * (s + 1) + last * (lax.rem(zh + 1, 4) * 4 + q)
+            place = q + last * (4 - q) if q > 0 else 0
+            rdma(pieces(q), buf.at[place], ss.at[q], rs.at[place], (dest, j)).start()
+
+    def go_down(pieces, buf, ss, rs):
+        for q in range(4):
+            dest = (1 - first) * (s - 1) + first * (lax.rem(zh + 3, 4) * 4 + q)
+            place = q + first * (4 - q) if q < 3 else 3
+            rdma(pieces(q), buf.at[place], ss.at[q], rs.at[place], (dest, j)).start()
+
+    def pass_up(buf, ss, rs):
+        @pl.when(x > 0)
+        def _():
+            rdma(buf.at[4], buf.at[4], ss.at[4], rs.at[4], sib).wait_recv()
+            rdma(buf.at[4], buf.at[x], ss.at[4], rs.at[x], (zh * 4, j)).start()
+
+    def pass_down(buf, ss, rs):
+        @pl.when(x < 3)
+        def _():
+            rdma(buf.at[4], buf.at[4], ss.at[4], rs.at[4], sib).wait_recv()
+            rdma(buf.at[4], buf.at[x], ss.at[4], rs.at[x], (zh * 4 + 3, j)).start()
+
+    def arrived(buf, ss, rs):
+        for q in range(4):
+            rdma(buf.at[q], buf.at[q], ss.at[q], rs.at[q], sib).wait_recv()
+
+    def departed(buf, ss, rs, relayed):
+        for q in range(4):
+            rdma(buf.at[q], buf.at[q], ss.at[q], rs.at[q], sib).wait_send()
+
+        @pl.when(relayed)
+        def _():
+            rdma(buf.at[4], buf.at[4], ss.at[4], rs.at[4], sib).wait_send()
+
+    stage_z(0)
 
     def send_tokens(k, carry):
         d = lax.rem(j + k, NSEQ)
@@ -141,57 +237,16 @@
     own_tok = pltpu.make_async_copy(hbuf.at[j], xbuf.at[j], lsem.at[2])
     own_tok.start()
 
-    def x_ship(kind, yo, q):
-        i = kind * 4 + yo
-        ship(q, xsend, i, xdev(1 if (kind, yo) in plus else -1))
-
-    q = slot(0, za)
-
-    @pl.when(odd)
-    def _():
-        landed(q)
-        ship(q, ysend, 0, ydev(1))
-        ship(q, ysend, 1, ydev(-1))
-        x_ship(0, 0, q)
-        ship(q, ssend, 1, sib)
-
-    q1 = slot(0, zb)
-    landed(q1)
-    ship(q1, ysend, 2, ydev(1))
-    ship(q1, ysend, 3, ydev(-1))
-    x_ship(1, 0, q1)
-    ship(q1, ssend, 2, sib)
-    n = 3
-    for kind, yo in ((0, 3), (0, 1), (1, 1), (1, 3), (0, 2), (1, 2)):
-        q = slot(yo, zb if kind else za)
-        landed(q)
-        if (kind, yo) == (0, 3):
-            ship(q, ysend, 4, ydev(1))
-        if (kind, yo) == (1, 1):
-            ship(q, ysend, 5, ydev(-1))
-        x_ship(kind, yo, q)
-        ship(q, ssend, n, sib)
-        n += 1
-
-    q0 = slot(0, oa)
-
-    @pl.when(even)
-    def _():
-        landed(q0)
-        ship(q0, ssend, 1, sib)
-
-    for kind, yo in ((1, 0), (0, 1), (0, 3), (1, 1), (1, 3), (0, 2), (1, 2)):
-        q = slot(yo, ob if kind else oa)
-        landed(q)
-        ship(q, ssend, n, sib)
-        n += 1
+    stage_z(1)
+    stage_ab(0)
+    stage_y(0, near, 3)
+    stage_y(0, far, 7)
+    stage_ab(1)
 
     own_tok.wait()
     rdma(xbuf.at[pl.ds(0, NSEQ - 1)], xbuf.at[pl.ds(0, NSEQ - 1)], tsend, trecv, sib).wait_recv()
-    half_up = rdma(xbuf.at[pl.ds(16, 16), 0], halo_l, hsem.at[0], hsem.at[1], up)
-    half_down = rdma(xbuf.at[pl.ds(0, 16), 1], halo_u, hsem.at[2], hsem.at[3], down)
-    half_up.start()
-    half_down.start()
+    go_up(lambda q: xbuf.at[pl.ds(16 + 4 * q, 4), 0], halo_l, hsend.at[0], hrecv.at[0])
+    go_down(lambda q: xbuf.at[pl.ds(4 * q, 4), 1], halo_u, hsend.at[1], hrecv.at[1])
 
     for b in range(2):
         rows = xbuf[:, b].astype(F32).reshape(256, D).astype(BF)
@@ -199,14 +254,14 @@
     xb[128:256, :] = xa[0:128, :]
     xb[256:384, :] = xa[384:512, :]
 
-    def other(i, carry):
-        landed(i * 2 + 1 - c)
-        return carry
-
-    lax.fori_loop(0, 16, other, 0)
+    stage_y(1, near, 3)
+    stage_x(0)
+    pass_up(halo_l, hsend.at[0], hrecv.at[0])
+    pass_down(halo_u, hsend.at[1], hrecv.at[1])
+    stage_y(1, far, 7)
+    stage_s(0)
     for i in range(16):
         wt[216 * i:216 * i + 216, :] = jnp.concatenate([wq[2 * i], wq[2 * i + 1]], axis=0)
-        wot[72 * i:72 * i + 72, :] = jnp.concatenate([wo[2 * i], wo[2 * i + 1]], axis=0)
 
     def project(g, rows_ref):
         base = 1728 * g
@@ -268,54 +323,66 @@
     project(0, xa)
     attend(0, store_a)
 
-    half_up.wait()
-    half_down.wait()
-    xb[0:128, :] = halo_l[...].astype(F32).reshape(128, D).astype(BF)
-    xb[384:512, :] = halo_u[...].astype(F32).reshape(128, D).astype(BF)
+    stage_x(1)
+    arrived(halo_l, hsend.at[0], hrecv.at[0])
+    arrived(halo_u, hsend.at[1], hrecv.at[1])
+    xb[0:128, :] = halo_l[0:4].astype(F32).reshape(128, D).astype(BF)
+    xb[384:512, :] = halo_u[0:4].astype(F32).reshape(128, D).astype(BF)
     project(1, xb)
     attend(1, store_b)
 
-    back_l = rdma(att_b.at[pl.ds(0, 128)], ret_l, rsem.at[0], rsem.at[1], down)
-    back_u = rdma(att_b.at[pl.ds(384, 128)], ret_u, rsem.at[2], rsem.at[3], up)
-    back_l.start()
-    back_u.start()
-    back_l.wait()
-    back_u.wait()
-    for rows, part in (
-        (slice(0, 128), att_b[128:256, :]),
-        (slice(128, 256), ret_l[...]),
-        (slice(256, 384), ret_u[...]),
-        (slice(384, 512), att_b[256:384, :]),
-    ):
+    go_down(lambda q: att_b.at[pl.ds(32 * q, 32)], ret_l, hsend.at[2], hrecv.at[2])
+    go_up(lambda q: att_b.at[pl.ds(384 + 32 * q, 32)], ret_u, hsend.at[3], hrecv.at[3])
+
+    stage_s(1)
+    for i in range(16):
+        wot[72 * i:72 * i + 72, :] = jnp.concatenate([wo[2 * i], wo[2 * i + 1]], axis=0)
+
+    def finish(rows, part):
         att[rows, 512:640] = edge[rows, :] + part[:, 0:128]
         att[rows, 640:1152] = part[:, 128:640]
-
-    for b in range(2):
-        result = dot_nt(att[256 * b:256 * b + 256, :], wot[...])
-        obuf[:, b] = result.reshape(32, 8, D).astype(BF)
-
-    def send_out(k, carry):
-        d = lax.rem(j + k, NSEQ)
-        rdma(obuf.at[d], out_ref.at[j], osend, orecv, (s, d)).start()
-        return carry
-
-    lax.fori_loop(1, NSEQ, send_out, 0)
+        return dot_nt(att[rows, :], wot[...]).reshape(16, 8, D).astype(BF)
+
+    def send_half(low, high):
+        def send_out(k, carry):
+            d = lax.rem(j + k, NSEQ)
+            b = lax.div(d, 16) * (high - low) + low
+            rdma(obuf.at[d, b], out_ref.at[j, b], osend, orecv, (s, d)).start()
+            return carry
+
+        lax.fori_loop(1, NSEQ, send_out, 0)
+
+    obuf[0:16, 0] = finish(slice(0, 128), att_b[128:256, :])
+    obuf[16:32, 1] = finish(slice(384, 512), att_b[256:384, :])
+    send_half(0, 1)
+    pass_down(ret_l, hsend.at[2], hrecv.at[2])
+    pass_up(ret_u, hsend.at[3], hrecv.at[3])
+    arrived(ret_l, hsend.at[2], hrecv.at[2])
+    obuf[16:32, 0] = finish(slice(128, 256), ret_l[0:4].reshape(128, WIDE))
+    arrived(ret_u, hsend.at[3], hrecv.at[3])
+    obuf[0:16, 1] = finish(slice(256, 384), ret_u[0:4].reshape(128, WIDE))
+    send_half(1, 0)
     own_out = pltpu.make_async_copy(obuf.at[j], out_ref.at[j], lsem.at[2])
     own_out.start()
 
-    shipped(zsend, 0)
-
-    @pl.when(odd)
-    def _():
-        shipped(zsend, 1)
-        shipped(xsend, 0)
-
-    for i in range(6):
-        shipped(ysend, i)
-    for i in range(1, 8):
-        shipped(xsend, i)
-    for i in range(16):
-        shipped(ssend, i)
+    for t in range(2):
+        shipped(t, zsend, 0)
+
+        @pl.when(odd)
+        def _():
+            shipped(t, zsend, 1)
+            shipped(t, xsend, 0)
+
+        for i in range(6):
+            shipped(t, ysend, i)
+        for i in range(1, 8):
+            shipped(t, xsend, i)
+        for i in range(16):
+            shipped(t, ssend, i)
+    departed(halo_l, hsend.at[0], hrecv.at[0], x > 0)
+    departed(halo_u, hsend.at[1], hrecv.at[1], x < 3)
+    departed(ret_l, hsend.at[2], hrecv.at[2], x < 3)
+    departed(ret_u, hsend.at[3], hrecv.at[3], x > 0)
     own_out.wait()
     many = pl.ds(0, NSEQ - 1)
     rdma(hbuf.at[many], xbuf.at[many], tsend, trecv, sib).wait_send()
@@ -340,16 +407,16 @@
             pltpu.VMEM((D, D), BF),
             pltpu.VMEM((512, D), BF),
             pltpu.VMEM((512, D), BF),
-            pltpu.VMEM((16, 8, D), BF),
-            pltpu.VMEM((16, 8, D), BF),
+            pltpu.VMEM((5, 4, 8, D), BF),
+            pltpu.VMEM((5, 4, 8, D), BF),
             pltpu.VMEM((512, WIDE), BF),
             pltpu.VMEM((WIDE, 512), BF),
             pltpu.VMEM((512, WIDE), BF),
             pltpu.VMEM((512, D), BF),
             pltpu.VMEM((512, WIDE), BF),
             pltpu.VMEM((512, 128), BF),
-            pltpu.VMEM((128, WIDE), BF),
-            pltpu.VMEM((128, WIDE), BF),
+            pltpu.VMEM((5, 32, WIDE), BF),
+            pltpu.VMEM((5, 32, WIDE), BF),
             pltpu.VMEM((NSEQ, 2, 8, D), BF),
             pltpu.SemaphoreType.DMA((2, NSEQ)),
             pltpu.SemaphoreType.DMA((2, 2)),
@@ -359,8 +426,8 @@
             pltpu.SemaphoreType.DMA((3,)),
             pltpu.SemaphoreType.DMA,
             pltpu.SemaphoreType.DMA,
-            pltpu.SemaphoreType.DMA((4,)),
-            pltpu.SemaphoreType.DMA((4,)),
+            pltpu.SemaphoreType.DMA((4, 5)),
+            pltpu.SemaphoreType.DMA((4, 5)),
             pltpu.SemaphoreType.DMA,
             pltpu.SemaphoreType.DMA,
         ],
@@ -369,7 +436,7 @@
         ),
     )(
         video_tokens.reshape(512, D),
-        modulation.reshape(3, D),
+        modulation.transpose(1, 0, 2),
         qkv_weight.T,
         out_weight.T,
     )

time: 147 us -> 126 us (0.86); the launches traced: 145 us -> 126 us
  Pallas kernels: 140 us -> 122 us
    pallas_call x1, Pallas kernels: 140 us -> 122 us  [per_device(): pl.pallas_call(kernel, out_shape=jax.ShapeDtypeStruct((NSEQ, 2, 8, D), BF...]
where the time goes in v2:
time: 126 us
  Pallas kernels  122 us (97%)
  other arithmetic  2.64 us (2%)
    pallas_call x1, Pallas kernels, per_device(): pl.pallas_call(kernel, out_shape=jax.ShapeDtypeStruct((NSEQ, 2, 8, D), BF...  122 us
    convert_element_type x1, other arithmetic, per_device(): return restored.astype(BF)  2.64 us

profile of v2, /device:TPU:1, one launch (start us, length us, event | category | flops | bytes accessed | tf_op | source)
XLA Modules:
  0.0 125.8 jit_solution(8245332234139072594)
XLA Ops:
  0.0 0.7 slice_reduce_fusion
  0.7 0.0 copy-start
  0.7 122.4 %shard_map.46 = bf16[32,2,8,1152]{3,2,1,0:T(8,128)(2,1)} custom-call(bf16[512,1152]{1,0:T(8,128)(2,1)} %bitcast.6, f32[3,1,1152]{2,1,0:T(1,128)} %bitcast.10, bf16[108,1152]{1,0:T(8,128)(2,1)} %bitcast.8, bf16[36,1152]{1,0:T(8,128)(2,1)} %bitcast.9), custom_call_target="tpu_custom_call" | custom-call | tf_op jit(solution)/shard_map/pallas_call | solution.py:396
  123.2 0.0 copy-done
  123.2 2.6 %fusion.1 = bf16[1,512,1152]{2,1,0:T(8,128)(2,1)} fusion(bf16[1,512,1152]{2,1,0:T(8,128)(2,1)} %bitcast.7, bf16[1,512,1152]{2,1,0:T(8,128)(2,1)S(1)} %copy-done, f32[1152]{0:T(1024)S(1)} %slice_reduce_fusion), kind=kLoop, calls=%fused_computation.2 | loop fusion | flops 2949120 | bytes 3543552 | tf_op jit(solution)/shard_map/convert_element_type | solution.py:445
Async XLA Ops:
  0.7 122.5 %copy-start = (bf16[1,512,1152]{2,1,0:T(8,128)(2,1)S(1)}, bf16[1,512,1152]{2,1,0:T(8,128)(2,1)}, u32[]{:S(2)}) copy-start(bf16[1,512,1152]{2,1,0:T(8,128)(2,1)} %param.4) | copy-start | bytes 3538948

commit v3 on v2

--- a/solution.py
+++ b/solution.py
@@ -100,16 +100,19 @@
     def slot(yo, zo):
         return lax.rem(y + yo, 4) * 8 + lax.rem(zl + zo, 4) * 2 + c
 
-    bufs = (wq, wo)
+    def part(t, q):
+        if t == 2:
+            return wo.at[q]
+        return wq.at[q, :, pl.ds(0, 640)] if t == 0 else wq.at[q, :, pl.ds(640, 512)]
 
     def ship(t, q, sems, i, dev):
-        rdma(bufs[t].at[q], bufs[t].at[q], sems.at[t, i], wrecv.at[t, q], dev).start()
+        rdma(part(t, q), part(t, q), sems.at[t, i], wrecv.at[t, q], dev).start()
 
     def shipped(t, sems, i):
-        rdma(bufs[t].at[0], bufs[t].at[0], sems.at[t, i], wrecv.at[t, 0], sib).wait_send()
+        rdma(part(t, 0), part(t, 0), sems.at[t, i], wrecv.at[t, 0], sib).wait_send()
 
     def landed(t, q):
-        rdma(bufs[t].at[q], bufs[t].at[q], zsend.at[t, 0], wrecv.at[t, q], sib).wait_recv()
+        rdma(part(t, q), part(t, q), zsend.at[t, 0], wrecv.at[t, q], sib).wait_recv()
 
     za = par * 3
     zb = 1 + par
@@ -192,27 +195,31 @@
 
     def go_up(pieces, buf, ss, rs):
         for q in range(4):
-            dest = (1 - last) * (s + 1) + last * (lax.rem(zh + 1, 4) * 4 + q)
-            place = q + last * (4 - q) if q > 0 else 0
+            far_slab = zh * 4 + q if q < 3 else lax.rem(zh + 1, 4) * 4
+            dest = (1 - last) * (s + 1) + last * far_slab
+            place = q + last * (4 - q) if q < 3 else 3
             rdma(pieces(q), buf.at[place], ss.at[q], rs.at[place], (dest, j)).start()
 
     def go_down(pieces, buf, ss, rs):
         for q in range(4):
-            dest = (1 - first) * (s - 1) + first * (lax.rem(zh + 3, 4) * 4 + q)
-            place = q + first * (4 - q) if q < 3 else 3
+            far_slab = zh * 4 + q if q > 0 else lax.rem(zh + 3, 4) * 4 + 3
+            dest = (1 - first) * (s - 1) + first * far_slab
+            place = q + first * (4 - q) if q > 0 else 0
             rdma(pieces(q), buf.at[place], ss.at[q], rs.at[place], (dest, j)).start()
 
     def pass_up(buf, ss, rs):
+        @pl.when(x < 3)
+        def _():
+            rdma(buf.at[4], buf.at[4], ss.at[4], rs.at[4], sib).wait_recv()
+            rdma(buf.at[4], buf.at[x], ss.at[4], rs.at[x], (lax.rem(zh + 1, 4) * 4, j)).start()
+
+    def pass_down(buf, ss, rs):
         @pl.when(x > 0)
         def _():
             rdma(buf.at[4], buf.at[4], ss.at[4], rs.at[4], sib).wait_recv()
-            rdma(buf.at[4], buf.at[x], ss.at[4], rs.at[x], (zh * 4, j)).start()
-
-    def pass_down(buf, ss, rs):
-        @pl.when(x < 3)
-        def _():
-            rdma(buf.at[4], buf.at[4], ss.at[4], rs.at[4], sib).wait_recv()
-            rdma(buf.at[4], buf.at[x], ss.at[4], rs.at[x], (zh * 4 + 3, j)).start()
+            rdma(
+                buf.at[4], buf.at[x], ss.at[4], rs.at[x], (lax.rem(zh + 3, 4) * 4 + 3, j)
+            ).start()
 
     def arrived(buf, ss, rs):
         for q in range(4):
@@ -227,6 +234,7 @@
             rdma(buf.at[4], buf.at[4], ss.at[4], rs.at[4], sib).wait_send()
 
     stage_z(0)
+    stage_z(1)
 
     def send_tokens(k, carry):
         d = lax.rem(j + k, NSEQ)
@@ -237,11 +245,14 @@
     own_tok = pltpu.make_async_copy(hbuf.at[j], xbuf.at[j], lsem.at[2])
     own_tok.start()
 
-    stage_z(1)
+    stage_z(2)
     stage_ab(0)
+    stage_ab(1)
     stage_y(0, near, 3)
+    stage_y(1, near, 3)
     stage_y(0, far, 7)
-    stage_ab(1)
+    stage_y(1, far, 7)
+    stage_ab(2)
 
     own_tok.wait()
     rdma(xbuf.at[pl.ds(0, NSEQ - 1)], xbuf.at[pl.ds(0, NSEQ - 1)], tsend, trecv, sib).wait_recv()
@@ -254,12 +265,14 @@
     xb[128:256, :] = xa[0:128, :]
     xb[256:384, :] = xa[384:512, :]
 
-    stage_y(1, near, 3)
-    stage_x(0)
     pass_up(halo_l, hsend.at[0], hrecv.at[0])
     pass_down(halo_u, hsend.at[1], hrecv.at[1])
-    stage_y(1, far, 7)
+    stage_x(0)
+    stage_x(1)
+    stage_y(2, near, 3)
+    stage_y(2, far, 7)
     stage_s(0)
+    stage_s(1)
     for i in range(16):
         wt[216 * i:216 * i + 216, :] = jnp.concatenate([wq[2 * i], wq[2 * i + 1]], axis=0)
 
@@ -323,7 +336,7 @@
     project(0, xa)
     attend(0, store_a)
 
-    stage_x(1)
+    stage_x(2)
     arrived(halo_l, hsend.at[0], hrecv.at[0])
     arrived(halo_u, hsend.at[1], hrecv.at[1])
     xb[0:128, :] = halo_l[0:4].astype(F32).reshape(128, D).astype(BF)
@@ -334,7 +347,7 @@
     go_down(lambda q: att_b.at[pl.ds(32 * q, 32)], ret_l, hsend.at[2], hrecv.at[2])
     go_up(lambda q: att_b.at[pl.ds(384 + 32 * q, 32)], ret_u, hsend.at[3], hrecv.at[3])
 
-    stage_s(1)
+    stage_s(2)
     for i in range(16):
         wot[72 * i:72 * i + 72, :] = jnp.concatenate([wo[2 * i], wo[2 * i + 1]], axis=0)
 
@@ -365,7 +378,7 @@
     own_out = pltpu.make_async_copy(obuf.at[j], out_ref.at[j], lsem.at[2])
     own_out.start()
 
-    for t in range(2):
+    for t in range(3):
         shipped(t, zsend, 0)
 
         @pl.when(odd)
@@ -379,10 +392,10 @@
             shipped(t, xsend, i)
         for i in range(16):
             shipped(t, ssend, i)
-    departed(halo_l, hsend.at[0], hrecv.at[0], x > 0)
-    departed(halo_u, hsend.at[1], hrecv.at[1], x < 3)
-    departed(ret_l, hsend.at[2], hrecv.at[2], x < 3)
-    departed(ret_u, hsend.at[3], hrecv.at[3], x > 0)
+    departed(halo_l, hsend.at[0], hrecv.at[0], x < 3)
+    departed(halo_u, hsend.at[1], hrecv.at[1], x > 0)
+    departed(ret_l, hsend.at[2], hrecv.at[2], x > 0)
+    departed(ret_u, hsend.at[3], hrecv.at[3], x < 3)
     own_out.wait()
     many = pl.ds(0, NSEQ - 1)
     rdma(hbuf.at[many], xbuf.at[many], tsend, trecv, sib).wait_send()
@@ -418,11 +431,11 @@
             pltpu.VMEM((5, 32, WIDE), BF),
             pltpu.VMEM((5, 32, WIDE), BF),
             pltpu.VMEM((NSEQ, 2, 8, D), BF),
-            pltpu.SemaphoreType.DMA((2, NSEQ)),
-            pltpu.SemaphoreType.DMA((2, 2)),
-            pltpu.SemaphoreType.DMA((2, 6)),
-            pltpu.SemaphoreType.DMA((2, 8)),
-            pltpu.SemaphoreType.DMA((2, 16)),
+            pltpu.SemaphoreType.DMA((3, NSEQ)),
+            pltpu.SemaphoreType.DMA((3, 2)),
+            pltpu.SemaphoreType.DMA((3, 6)),
+            pltpu.SemaphoreType.DMA((3, 8)),
+            pltpu.SemaphoreType.DMA((3, 16)),
             pltpu.SemaphoreType.DMA((3,)),
             pltpu.SemaphoreType.DMA,
             pltpu.SemaphoreType.DMA,

time: 126 us -> 130 us (1.032); the launches traced: 126 us -> 128 us
  Pallas kernels: 122 us -> 125 us
    pallas_call x1, Pallas kernels: 122 us -> 125 us  [per_device(): pl.pallas_call(kernel, out_shape=jax.ShapeDtypeStruct((NSEQ, 2, 8, D), BF...]
where the time goes in v3:
time: 130 us; the launch traced here: 128 us
  Pallas kernels  125 us (96%)
  other arithmetic  2.64 us (2%)
    pallas_call x1, Pallas kernels, per_device(): pl.pallas_call(kernel, out_shape=jax.ShapeDtypeStruct((NSEQ, 2, 8, D), BF...  125 us
    convert_element_type x1, other arithmetic, per_device(): return restored.astype(BF)  2.64 us

profile of v3, /device:TPU:1, one launch (start us, length us, event | category | flops | bytes accessed | tf_op | source)
XLA Modules:
  0.0 128.0 jit_solution(7784580041257922250)
XLA Ops:
  0.0 0.7 slice_reduce_fusion
  0.7 0.0 copy-start
  0.7 124.7 %shard_map.46 = bf16[32,2,8,1152]{3,2,1,0:T(8,128)(2,1)} custom-call(bf16[512,1152]{1,0:T(8,128)(2,1)} %bitcast.6, f32[3,1,1152]{2,1,0:T(1,128)} %bitcast.10, bf16[108,1152]{1,0:T(8,128)(2,1)} %bitcast.8, bf16[36,1152]{1,0:T(8,128)(2,1)} %bitcast.9), custom_call_target="tpu_custom_call" | custom-call | tf_op jit(solution)/shard_map/pallas_call | solution.py:409
  125.4 0.0 copy-done
  125.4 2.6 %fusion.1 = bf16[1,512,1152]{2,1,0:T(8,128)(2,1)} fusion(bf16[1,512,1152]{2,1,0:T(8,128)(2,1)} %bitcast.7, bf16[1,512,1152]{2,1,0:T(8,128)(2,1)S(1)} %copy-done, f32[1152]{0:T(1024)S(1)} %slice_reduce_fusion), kind=kLoop, calls=%fused_computation.2 | loop fusion | flops 2949120 | bytes 3543552 | tf_op jit(solution)/shard_map/convert_element_type | solution.py:458
Async XLA Ops:
  0.7 124.7 %copy-start = (bf16[1,512,1152]{2,1,0:T(8,128)(2,1)S(1)}, bf16[1,512,1152]{2,1,0:T(8,128)(2,1)}, u32[]{:S(2)}) copy-start(bf16[1,512,1152]{2,1,0:T(8,128)(2,1)} %param.4) | copy-start | bytes 3538948

commit v4 on v3

--- a/solution.py
+++ b/solution.py
@@ -132,7 +132,7 @@
 
         @pl.when(odd)
         def _():
-            ship(t, j, zsend, 1, zdev(-2))
+            ship(t, j, zsend, 1, zdev(lax.div(zl, 2) * 4 - 2))
             ship(t, j, zsend, 0, zdev(1))
 
         ship(t, j, ssend, 0, sib)
@@ -236,23 +236,28 @@
     stage_z(0)
     stage_z(1)
 
-    def send_tokens(k, carry):
-        d = lax.rem(j + k, NSEQ)
-        rdma(hbuf.at[d], xbuf.at[j], tsend, trecv, (s, d)).start()
-        return carry
-
-    lax.fori_loop(1, NSEQ, send_tokens, 0)
+    def send_tokens(yo):
+        def send(k, carry):
+            d = lax.rem(y + yo, 4) * 8 + lax.rem(zl * 2 + c + k, 8)
+            rdma(hbuf.at[d], xbuf.at[j], tsend, trecv, (s, d)).start()
+            return carry
+
+        lax.fori_loop(0 if yo else 1, 8, send, 0)
+
+    send_tokens(0)
+    send_tokens(1)
+    send_tokens(3)
     own_tok = pltpu.make_async_copy(hbuf.at[j], xbuf.at[j], lsem.at[2])
     own_tok.start()
 
-    stage_z(2)
     stage_ab(0)
     stage_ab(1)
+    send_tokens(2)
     stage_y(0, near, 3)
     stage_y(1, near, 3)
+    stage_z(2)
     stage_y(0, far, 7)
     stage_y(1, far, 7)
-    stage_ab(2)
 
     own_tok.wait()
     rdma(xbuf.at[pl.ds(0, NSEQ - 1)], xbuf.at[pl.ds(0, NSEQ - 1)], tsend, trecv, sib).wait_recv()
@@ -265,16 +270,16 @@
     xb[128:256, :] = xa[0:128, :]
     xb[256:384, :] = xa[384:512, :]
 
-    pass_up(halo_l, hsend.at[0], hrecv.at[0])
-    pass_down(halo_u, hsend.at[1], hrecv.at[1])
+    stage_ab(2)
     stage_x(0)
     stage_x(1)
-    stage_y(2, near, 3)
-    stage_y(2, far, 7)
     stage_s(0)
     stage_s(1)
     for i in range(16):
         wt[216 * i:216 * i + 216, :] = jnp.concatenate([wq[2 * i], wq[2 * i + 1]], axis=0)
+    pass_up(halo_l, hsend.at[0], hrecv.at[0])
+    pass_down(halo_u, hsend.at[1], hrecv.at[1])
+    stage_y(2, near, 3)
 
     def project(g, rows_ref):
         base = 1728 * g
@@ -334,14 +339,14 @@
         att_b[at, t * 128:t * 128 + 128] = value
 
     project(0, xa)
+    stage_y(2, far, 7)
     attend(0, store_a)
-
-    stage_x(2)
     arrived(halo_l, hsend.at[0], hrecv.at[0])
     arrived(halo_u, hsend.at[1], hrecv.at[1])
     xb[0:128, :] = halo_l[0:4].astype(F32).reshape(128, D).astype(BF)
     xb[384:512, :] = halo_u[0:4].astype(F32).reshape(128, D).astype(BF)
     project(1, xb)
+    stage_x(2)
     attend(1, store_b)
 
     go_down(lambda q: att_b.at[pl.ds(32 * q, 32)], ret_l, hsend.at[2], hrecv.at[2])
@@ -367,9 +372,9 @@
 
     obuf[0:16, 0] = finish(slice(0, 128), att_b[128:256, :])
     obuf[16:32, 1] = finish(slice(384, 512), att_b[256:384, :])
-    send_half(0, 1)
     pass_down(ret_l, hsend.at[2], hrecv.at[2])
     pass_up(ret_u, hsend.at[3], hrecv.at[3])
+    send_half(0, 1)
     arrived(ret_l, hsend.at[2], hrecv.at[2])
     obuf[16:32, 0] = finish(slice(128, 256), ret_l[0:4].reshape(128, WIDE))
     arrived(ret_u, hsend.at[3], hrecv.at[3])

time: 130 us -> 118 us (0.908)
  the two profiles are of different devices: /device:TPU:1 before, /device:TPU:67 now
where the time goes in v4:
time: 118 us; the launch traced here: 117 us
  Pallas kernels  114 us (97%)
  other arithmetic  2.64 us (2%)
    pallas_call x1, Pallas kernels, per_device(): pl.pallas_call(kernel, out_shape=jax.ShapeDtypeStruct((NSEQ, 2, 8, D), BF...  114 us
    convert_element_type x1, other arithmetic, per_device(): return restored.astype(BF)  2.64 us

profile of v4, /device:TPU:67, one launch (start us, length us, event | category | flops | bytes accessed | tf_op | source)
XLA Modules:
  0.0 117.4 jit_solution(17282721727553194813)
XLA Ops:
  0.0 0.7 slice_reduce_fusion
  0.7 0.0 copy-start
  0.7 114.0 %shard_map.46 = bf16[32,2,8,1152]{3,2,1,0:T(8,128)(2,1)} custom-call(bf16[512,1152]{1,0:T(8,128)(2,1)} %bitcast.6, f32[3,1,1152]{2,1,0:T(1,128)} %bitcast.10, bf16[108,1152]{1,0:T(8,128)(2,1)} %bitcast.8, bf16[36,1152]{1,0:T(8,128)(2,1)} %bitcast.9), custom_call_target="tpu_custom_call" | custom-call | tf_op jit(solution)/shard_map/pallas_call | solution.py:414
  114.8 0.0 copy-done
  114.8 2.6 %fusion.1 = bf16[1,512,1152]{2,1,0:T(8,128)(2,1)} fusion(bf16[1,512,1152]{2,1,0:T(8,128)(2,1)} %bitcast.7, bf16[1,512,1152]{2,1,0:T(8,128)(2,1)S(1)} %copy-done, f32[1152]{0:T(1024)S(1)} %slice_reduce_fusion), kind=kLoop, calls=%fused_computation.2 | loop fusion | flops 2949120 | bytes 3543552 | tf_op jit(solution)/shard_map/convert_element_type | solution.py:463
Async XLA Ops:
  0.7 114.1 %copy-start = (bf16[1,512,1152]{2,1,0:T(8,128)(2,1)S(1)}, bf16[1,512,1152]{2,1,0:T(8,128)(2,1)}, u32[]{:S(2)}) copy-start(bf16[1,512,1152]{2,1,0:T(8,128)(2,1)} %param.4) | copy-start | bytes 3538948

commit v5 on v4

--- a/solution.py
+++ b/solution.py
@@ -121,7 +121,8 @@
     plus = ((0, 0), (0, 2), (1, 1), (1, 3))
 
     def x_ship(t, kind, yo, q):
-        ship(t, q, xsend, kind * 4 + yo, xdev(1 if (kind, yo) in plus else -1))
+        right = t == 0 or (t == 2 and (kind, yo) in plus)
+        ship(t, q, xsend, kind * 4 + yo, xdev(1 if right else -1))
 
     def stage_z(t):
         @pl.when(even)
@@ -255,9 +256,9 @@
     send_tokens(2)
     stage_y(0, near, 3)
     stage_y(1, near, 3)
-    stage_z(2)
     stage_y(0, far, 7)
     stage_y(1, far, 7)
+    stage_z(2)
 
     own_tok.wait()
     rdma(xbuf.at[pl.ds(0, NSEQ - 1)], xbuf.at[pl.ds(0, NSEQ - 1)], tsend, trecv, sib).wait_recv()
@@ -270,9 +271,9 @@
     xb[128:256, :] = xa[0:128, :]
     xb[256:384, :] = xa[384:512, :]
 
-    stage_ab(2)
     stage_x(0)
     stage_x(1)
+    stage_ab(2)
     stage_s(0)
     stage_s(1)
     for i in range(16):
@@ -339,8 +340,8 @@
         att_b[at, t * 128:t * 128 + 128] = value
 
     project(0, xa)
+    attend(0, store_a)
     stage_y(2, far, 7)
-    attend(0, store_a)
     arrived(halo_l, hsend.at[0], hrecv.at[0])
     arrived(halo_u, hsend.at[1], hrecv.at[1])
     xb[0:128, :] = halo_l[0:4].astype(F32).reshape(128, D).astype(BF)
@@ -361,25 +362,27 @@
         att[rows, 640:1152] = part[:, 128:640]
         return dot_nt(att[rows, :], wot[...]).reshape(16, 8, D).astype(BF)
 
-    def send_half(low, high):
-        def send_out(k, carry):
-            d = lax.rem(j + k, NSEQ)
-            b = lax.div(d, 16) * (high - low) + low
-            rdma(obuf.at[d, b], out_ref.at[j, b], osend, orecv, (s, d)).start()
-            return carry
-
-        lax.fori_loop(1, NSEQ, send_out, 0)
+    def send_half(low, high, steps):
+        for yo in steps:
+            def send_out(k, carry, yo=yo):
+                d = lax.rem(y + yo, 4) * 8 + lax.rem(zl * 2 + c + k, 8)
+                b = lax.div(d, 16) * (high - low) + low
+                rdma(obuf.at[d, b], out_ref.at[j, b], osend, orecv, (s, d)).start()
+                return carry
+
+            lax.fori_loop(0 if yo else 1, 8, send_out, 0)
 
     obuf[0:16, 0] = finish(slice(0, 128), att_b[128:256, :])
     obuf[16:32, 1] = finish(slice(384, 512), att_b[256:384, :])
+    send_half(0, 1, (0,))
     pass_down(ret_l, hsend.at[2], hrecv.at[2])
     pass_up(ret_u, hsend.at[3], hrecv.at[3])
-    send_half(0, 1)
+    send_half(0, 1, (2, 1, 3))
     arrived(ret_l, hsend.at[2], hrecv.at[2])
     obuf[16:32, 0] = finish(slice(128, 256), ret_l[0:4].reshape(128, WIDE))
     arrived(ret_u, hsend.at[3], hrecv.at[3])
     obuf[0:16, 1] = finish(slice(256, 384), ret_u[0:4].reshape(128, WIDE))
-    send_half(1, 0)
+    send_half(1, 0, (2, 1, 3, 0))
     own_out = pltpu.make_async_copy(obuf.at[j], out_ref.at[j], lsem.at[2])
     own_out.start()
 

time: 118 us -> 118 us (level)
  the two profiles are of different devices: /device:TPU:67 before, /device:TPU:1 now
where the time goes in v5:
time: 118 us; the launch traced here: 116 us
  Pallas kernels  113 us (96%)
  other arithmetic  2.64 us (2%)
    pallas_call x1, Pallas kernels, per_device(): pl.pallas_call(kernel, out_shape=jax.ShapeDtypeStruct((NSEQ, 2, 8, D), BF...  113 us
    convert_element_type x1, other arithmetic, per_device(): return restored.astype(BF)  2.64 us

profile of v5, /device:TPU:1, one launch (start us, length us, event | category | flops | bytes accessed | tf_op | source)
XLA Modules:
  0.0 116.3 jit_solution(14799013413735573712)
XLA Ops:
  0.0 0.7 slice_reduce_fusion
  0.7 0.0 copy-start
  0.7 113.0 %shard_map.46 = bf16[32,2,8,1152]{3,2,1,0:T(8,128)(2,1)} custom-call(bf16[512,1152]{1,0:T(8,128)(2,1)} %bitcast.6, f32[3,1,1152]{2,1,0:T(1,128)} %bitcast.10, bf16[108,1152]{1,0:T(8,128)(2,1)} %bitcast.8, bf16[36,1152]{1,0:T(8,128)(2,1)} %bitcast.9), custom_call_target="tpu_custom_call" | custom-call | tf_op jit(solution)/shard_map/pallas_call | solution.py:417
  113.7 0.0 copy-done
  113.7 2.6 %fusion.1 = bf16[1,512,1152]{2,1,0:T(8,128)(2,1)} fusion(bf16[1,512,1152]{2,1,0:T(8,128)(2,1)} %bitcast.7, bf16[1,512,1152]{2,1,0:T(8,128)(2,1)S(1)} %copy-done, f32[1152]{0:T(1024)S(1)} %slice_reduce_fusion), kind=kLoop, calls=%fused_computation.2 | loop fusion | flops 2949120 | bytes 3543552 | tf_op jit(solution)/shard_map/convert_element_type | solution.py:466
Async XLA Ops:
  0.7 113.0 %copy-start = (bf16[1,512,1152]{2,1,0:T(8,128)(2,1)S(1)}, bf16[1,512,1152]{2,1,0:T(8,128)(2,1)}, u32[]{:S(2)}) copy-start(bf16[1,512,1152]{2,1,0:T(8,128)(2,1)} %param.4) | copy-start | bytes 3538948

commit v6 on v5

--- a/solution.py
+++ b/solution.py
@@ -124,12 +124,16 @@
         right = t == 0 or (t == 2 and (kind, yo) in plus)
         ship(t, q, xsend, kind * 4 + yo, xdev(1 if right else -1))
 
+    def own_y(t):
+        ship(t, j, ysend, 0, ydev(1))
+        ship(t, j, ysend, 1, ydev(-1))
+
     def stage_z(t):
         @pl.when(even)
         def _():
             ship(t, j, zsend, 0, zdev(-1))
-            ship(t, j, ysend, 0, ydev(1))
-            ship(t, j, ysend, 1, ydev(-1))
+            if t < 2:
+                own_y(t)
 
         @pl.when(odd)
         def _():
@@ -256,9 +260,9 @@
     send_tokens(2)
     stage_y(0, near, 3)
     stage_y(1, near, 3)
+    stage_z(2)
     stage_y(0, far, 7)
     stage_y(1, far, 7)
-    stage_z(2)
 
     own_tok.wait()
     rdma(xbuf.at[pl.ds(0, NSEQ - 1)], xbuf.at[pl.ds(0, NSEQ - 1)], tsend, trecv, sib).wait_recv()
@@ -271,15 +275,20 @@
     xb[128:256, :] = xa[0:128, :]
     xb[256:384, :] = xa[384:512, :]
 
+
+    @pl.when(even)
+    def _():
+        own_y(2)
+
+    stage_ab(2)
     stage_x(0)
     stage_x(1)
-    stage_ab(2)
+    pass_up(halo_l, hsend.at[0], hrecv.at[0])
+    pass_down(halo_u, hsend.at[1], hrecv.at[1])
     stage_s(0)
     stage_s(1)
     for i in range(16):
         wt[216 * i:216 * i + 216, :] = jnp.concatenate([wq[2 * i], wq[2 * i + 1]], axis=0)
-    pass_up(halo_l, hsend.at[0], hrecv.at[0])
-    pass_down(halo_u, hsend.at[1], hrecv.at[1])
     stage_y(2, near, 3)
 
     def project(g, rows_ref):

time: 118 us -> 116 us (0.983)
  the two profiles are of different devices: /device:TPU:1 before, /device:TPU:67 now
where the time goes in v6:
time: 116 us
  Pallas kernels  112 us (97%)
  other arithmetic  2.64 us (2%)
    pallas_call x1, Pallas kernels, per_device(): pl.pallas_call(kernel, out_shape=jax.ShapeDtypeStruct((NSEQ, 2, 8, D), BF...  112 us
    convert_element_type x1, other arithmetic, per_device(): return restored.astype(BF)  2.64 us

profile of v6, /device:TPU:67, one launch (start us, length us, event | category | flops | bytes accessed | tf_op | source)
XLA Modules:
  0.0 115.8 jit_solution(18134638294950650579)
XLA Ops:
  0.0 0.7 slice_reduce_fusion
  0.7 0.0 copy-start
  0.7 112.4 %shard_map.46 = bf16[32,2,8,1152]{3,2,1,0:T(8,128)(2,1)} custom-call(bf16[512,1152]{1,0:T(8,128)(2,1)} %bitcast.6, f32[3,1,1152]{2,1,0:T(1,128)} %bitcast.10, bf16[108,1152]{1,0:T(8,128)(2,1)} %bitcast.8, bf16[36,1152]{1,0:T(8,128)(2,1)} %bitcast.9), custom_call_target="tpu_custom_call" | custom-call | tf_op jit(solution)/shard_map/pallas_call | solution.py:426
  113.1 0.0 copy-done
  113.1 2.6 %fusion.1 = bf16[1,512,1152]{2,1,0:T(8,128)(2,1)} fusion(bf16[1,512,1152]{2,1,0:T(8,128)(2,1)} %bitcast.7, bf16[1,512,1152]{2,1,0:T(8,128)(2,1)S(1)} %copy-done, f32[1152]{0:T(1024)S(1)} %slice_reduce_fusion), kind=kLoop, calls=%fused_computation.2 | loop fusion | flops 2949120 | bytes 3543552 | tf_op jit(solution)/shard_map/convert_element_type | solution.py:475
Async XLA Ops:
  0.7 112.4 %copy-start = (bf16[1,512,1152]{2,1,0:T(8,128)(2,1)S(1)}, bf16[1,512,1152]{2,1,0:T(8,128)(2,1)}, u32[]{:S(2)}) copy-start(bf16[1,512,1152]{2,1,0:T(8,128)(2,1)} %param.4) | copy-start | bytes 3538948

commit v7 on v6

--- a/solution.py
+++ b/solution.py
@@ -137,21 +137,30 @@
 
         @pl.when(odd)
         def _():
+            ship(t, j, zsend, 0, zdev(1))
+
+        @pl.when(odd & (zl < 3))
+        def _():
             ship(t, j, zsend, 1, zdev(lax.div(zl, 2) * 4 - 2))
-            ship(t, j, zsend, 0, zdev(1))
 
         ship(t, j, ssend, 0, sib)
 
-    def stage_ab(t):
+    def stage_a(t):
         @pl.when(odd)
         def _():
             q = slot(0, za)
             landed(t, q)
+
+            @pl.when(zl == 0)
+            def _():
+                ship(t, q, zsend, 2, zdev(1))
+
             ship(t, q, ysend, 0, ydev(1))
             ship(t, q, ysend, 1, ydev(-1))
             x_ship(t, 0, 0, q)
             ship(t, q, ssend, 1, sib)
 
+    def stage_b(t):
         q = slot(0, zb)
         landed(t, q)
         ship(t, q, ysend, 2, ydev(1))
@@ -255,8 +264,10 @@
     own_tok = pltpu.make_async_copy(hbuf.at[j], xbuf.at[j], lsem.at[2])
     own_tok.start()
 
-    stage_ab(0)
-    stage_ab(1)
+    stage_a(0)
+    stage_a(1)
+    stage_b(0)
+    stage_b(1)
     send_tokens(2)
     stage_y(0, near, 3)
     stage_y(1, near, 3)
@@ -280,7 +291,8 @@
     def _():
         own_y(2)
 
-    stage_ab(2)
+    stage_a(2)
+    stage_b(2)
     stage_x(0)
     stage_x(1)
     pass_up(halo_l, hsend.at[0], hrecv.at[0])
@@ -400,8 +412,15 @@
 
         @pl.when(odd)
         def _():
+            shipped(t, xsend, 0)
+
+        @pl.when(odd & (zl < 3))
+        def _():
             shipped(t, zsend, 1)
-            shipped(t, xsend, 0)
+
+        @pl.when(odd & (zl == 0))
+        def _():
+            shipped(t, zsend, 2)
 
         for i in range(6):
             shipped(t, ysend, i)
@@ -449,7 +468,7 @@
             pltpu.VMEM((5, 32, WIDE), BF),
             pltpu.VMEM((NSEQ, 2, 8, D), BF),
             pltpu.SemaphoreType.DMA((3, NSEQ)),
-            pltpu.SemaphoreType.DMA((3, 2)),
+            pltpu.SemaphoreType.DMA((3, 3)),
             pltpu.SemaphoreType.DMA((3, 6)),
             pltpu.SemaphoreType.DMA((3, 8)),
             pltpu.SemaphoreType.DMA((3, 16)),

time: 116 us -> 116 us (level)
  the two profiles are of different devices: /device:TPU:67 before, /device:TPU:1 now
where the time goes in v7:
time: 116 us; the launch traced here: 115 us
  Pallas kernels  111 us (96%)
  other arithmetic  2.64 us (2%)
    pallas_call x1, Pallas kernels, per_device(): pl.pallas_call(kernel, out_shape=jax.ShapeDtypeStruct((NSEQ, 2, 8, D), BF...  111 us
    convert_element_type x1, other arithmetic, per_device(): return restored.astype(BF)  2.64 us

profile of v7, /device:TPU:1, one launch (start us, length us, event | category | flops | bytes accessed | tf_op | source)
XLA Modules:
  0.0 114.7 jit_solution(16350848492077918523)
XLA Ops:
  0.0 0.7 slice_reduce_fusion
  0.7 0.0 copy-start
  0.7 111.3 %shard_map.46 = bf16[32,2,8,1152]{3,2,1,0:T(8,128)(2,1)} custom-call(bf16[512,1152]{1,0:T(8,128)(2,1)} %bitcast.6, f32[3,1,1152]{2,1,0:T(1,128)} %bitcast.10, bf16[108,1152]{1,0:T(8,128)(2,1)} %bitcast.8, bf16[36,1152]{1,0:T(8,128)(2,1)} %bitcast.9), custom_call_target="tpu_custom_call" | custom-call | tf_op jit(solution)/shard_map/pallas_call | solution.py:445
  112.0 0.0 copy-done
  112.0 2.6 %fusion.1 = bf16[1,512,1152]{2,1,0:T(8,128)(2,1)} fusion(bf16[1,512,1152]{2,1,0:T(8,128)(2,1)} %bitcast.7, bf16[1,512,1152]{2,1,0:T(8,128)(2,1)S(1)} %copy-done, f32[1152]{0:T(1024)S(1)} %slice_reduce_fusion), kind=kLoop, calls=%fused_computation.2 | loop fusion | flops 2949120 | bytes 3543552 | tf_op jit(solution)/shard_map/convert_element_type | solution.py:494
Async XLA Ops:
  0.7 111.3 %copy-start = (bf16[1,512,1152]{2,1,0:T(8,128)(2,1)S(1)}, bf16[1,512,1152]{2,1,0:T(8,128)(2,1)}, u32[]{:S(2)}) copy-start(bf16[1,512,1152]{2,1,0:T(8,128)(2,1)} %param.4) | copy-start | bytes 3538948
